TPU v7x, 256 devices: a whole 4x4x8 slice. The times are simulated.
256 devices in a mesh: order: 16 (over x_hi, z), blk: 16 (over y, x_lo, core).
Axes of the slice: x: 4 (x_hi: 2, x_lo: 2; x = x_hi * 2 + x_lo), y: 4, z: 8, core: 2. Of those that a mesh axis runs over, the one named last changes fastest.
Arguments:
- fourier_cycles: float32 [32, 512, 128], P('order', 'blk'), parts along dimension 0, may hold values from -6 to 6
- legendre: float32 [32, 512, 12288], P('order', 'blk'), parts along dimension 0, may hold values from -0.25 to 0.25
- cycle_weight: float32 [512], P('blk'), may hold values from 0.5 to 2
- matched_filter_weights: float32 [12288, 8, 8], P('blk'), may hold values from -2 to 2
- cluster_cycles: int32 [32, 64], P('order'), parts along dimension 0, may hold values from 0 to 511
- cluster_flux: float32 [32, 64, 128], P('order'), parts along dimension 0, may hold values from -18 to 18
- order_per_slot: int32 [32], P('order'), parts along dimension 0, may hold values from 0 to 6143
Outputs:
- synthesized: float32 [32, 512, 128], P('order', 'blk'), parts along dimension 0
There are 16 independent parts, one for each index of `order`. A program takes and returns all parts, laid end to end along the dimension named above; an argument that names none is the same for every part. Nothing has to cross between parts.
Inputs may be any that keep to these rules, and one draw needn't show every extreme that they name: `cluster_cycles`: cycle indices; several clusters may share a cycle, and their coefficients add. `order_per_slot`: order of each slot; degrees below it carry no coefficients.
All inputs are finite; a program needn't handle non-finite values.
Results may differ from a plain program's by a relative error of at most 0.00011.
Values sent between devices are 32-bit elements; how exact they have to be, the bound alone decides.
A program may use at most 128 MiB of HBM per device.

v0:
```python
import jax
import jax.numpy as jnp
from jax import lax
from jax.sharding import PartitionSpec as P

L = 12288
F = 8
S = 8
SIMS = 8
M = 2
highest_degree = lax.Precision.HIGHEST


def inject(fourier_cycles, cycle_weight, cluster_cycles, cluster_flux):
    local = fourier_cycles.shape[1]
    cycle_ids = lax.axis_index("blk") * local + lax.iota(jnp.int32, local)
    cycle_hits = (cycle_ids[None, :, None] == cluster_cycles[:, None, :]).astype(jnp.float32)
    added = jnp.einsum("krj,kjc->krc", cycle_hits, cluster_flux, precision=highest_degree)
    return cycle_weight[None, :, None] * (fourier_cycles + added)


def finish(owned, matched_filter_weights, order_per_slot):
    blocks = owned.shape[0]
    degrees = lax.axis_index("blk") * blocks + lax.iota(jnp.int32, blocks)
    harmonics = owned.reshape(blocks, M, 2 * F * SIMS)
    kept_mask = (degrees[:, None] >= order_per_slot[None, :]).astype(jnp.float32)
    masked_values = (harmonics * kept_mask[:, :, None]).reshape(blocks, M, 2, F, SIMS)
    matched_output = jnp.einsum(
        "dvr,dotrq->dotvq", matched_filter_weights, masked_values, precision=highest_degree
    )
    squares = jnp.sum(matched_filter_weights * matched_filter_weights, axis=2)
    weights = kept_mask * (2.0 * degrees.astype(jnp.float32) + 1.0)[:, None]
    response = jnp.einsum("lk,ls->ks", weights, squares, precision=highest_degree)
    response = lax.psum(response, "blk")
    scaled = matched_output * (L / jnp.sqrt(response))[None, :, None, :, None]
    return scaled.reshape(blocks, M, 2 * S * SIMS)


def body(
    fourier_cycles,
    legendre,
    cycle_weight,
    matched_filter_weights,
    cluster_cycles,
    cluster_flux,
    order_per_slot,
):
    injected = inject(fourier_cycles, cycle_weight, cluster_cycles, cluster_flux)
    orders_here = legendre.shape[0]
    width = injected.shape[2]
    blocks = legendre.shape[2] // lax.axis_size("blk")
    columns = legendre
    partial_running_sum = jnp.einsum("krl,krc->lkc", columns, injected, precision=highest_degree)
    owned = lax.psum_scatter(
        partial_running_sum.reshape(blocks * lax.axis_size("blk"), orders_here * width),
        "blk",
        scatter_dimension=0,
        tiled=True,
    )
    scaled = finish(owned, matched_filter_weights, order_per_slot)
    columns = legendre
    return jnp.einsum(
        "krl,lkc->krc",
        columns,
        lax.all_gather(scaled, "blk", axis=0, tiled=True),
        precision=highest_degree,
    )


def solution(mesh):
    return jax.shard_map(
        body,
        mesh=mesh,
        in_specs=(
            P("order", "blk", None),
            P("order", "blk", None),
            P("blk"),
            P("blk", None, None),
            P("order", None),
            P("order", None, None),
            P("order"),
        ),
        out_specs=P("order", "blk", None),
        check_vma=False,
    )
```

profile of v0, /device:TPU:1, one launch (start us, length us, event | category | flops | bytes accessed | tf_op | source)
XLA Modules:
  0.0 300.5 jit_solution(4388038787292911202)
XLA Ops:
  6.5 0.0 copy-start
  6.5 0.0 reduce-scatter.2.cloned.1.call-start
  6.5 1.2 fusion
  7.7 0.8 copy-done
  8.5 0.0 copy-start.1
  8.5 0.0 copy-start.2
  8.5 12.6 %fusion.10 = f32[2,128,12288]{2,1,0:T(8,128)} fusion(f32[2,32,128]{2,1,0:T(8,128)S(1)} %fusion, f32[2,32,12288]{2,1,0:T(8,128)S(1)} %copy-done), kind=kOutput, calls=%fused_computation.21 | convolution fusion | flops 1207959552 | bytes 15761408 | tf_op jit(solution)/shard_map/krl,krc->lkc/dot_general | solution.py:53
  21.1 0.0 reduce-scatter.2.cloned.1.call-update
  21.1 0.0 all-gather.2.cloned.1.call-start
  21.1 0.0 copy-done.1
  21.2 2.3 copy.17
  23.5 0.1 multiply_reduce_fusion
  23.5 0.0 copy-done.2
  23.5 0.2 fusion.4
  23.7 30.7 %psum.7 = f32[2,8]{1,0:T(2,128)S(1)} all-reduce(f32[2,8]{1,0:T(2,128)S(1)} %fusion.4), channel_id=1, replica_groups=mesh['order'=16,'blk'=16] {'blk'}, use_global_device_ids=true, to_apply=%region_2.0 | all-reduce | flops 16 | bytes 128 | tf_op jit(solution)/shard_map/psum | solution.py:34
  54.5 0.1 compare_convert_fusion
  54.5 111.8 %reduce-scatter.2.cloned.1.call-done = f32[768,256]{0,1:T(8,128)} async-done(((f32[12288,256]{0,1:T(8,128)}), f32[768,256]{0,1:T(8,128)}) %reduce-scatter.2.cloned.1.call-update) | async-done | bytes 786448 | tf_op jit(solution)/shard_map/reduce_scatter | solution.py:54
  166.3 2.1 broadcast_multiply_fusion
  168.4 11.3 %copy.13 = f32[768,2,2,8,8]{3,4,2,1,0:T(8,128)} copy(f32[768,2,2,8,8]{0,4,3,2,1:T(8,128)} %broadcast_multiply_fusion) | data formatting | bytes 1572864 | tf_op jit(solution)/shard_map/mul | solution.py:27
  179.8 16.1 %multiply_bitcast_fusion = f32[768,2,2,8,8]{3,4,2,1,0:T(8,128)} fusion(f32[2,8]{1,0:T(2,128)S(1)} %rsqrt_multiply_fusion, f32[768,2,2,8,8]{3,4,2,1,0:T(8,128)} %copy.13, f32[768,8,8,1,1]{2,1,4,3,0:T(8,128)} %copy.17), kind=kOutput, calls=%fused_computation | convolution fusion | flops 19070976 | bytes 1769536 | tf_op jit(solution)/shard_map/dvr,dotrq->dotvq/dot_general | solution.py:28
  195.8 9.9 %copy.15 = f32[768,2,2,8,8]{0,4,3,2,1:T(8,128)} copy(f32[768,2,2,8,8]{3,4,2,1,0:T(8,128)} %multiply_bitcast_fusion) | data formatting | bytes 1572864 | tf_op jit(solution)/shard_map/mul | solution.py:35
  205.8 2.3 copy.16
  208.1 0.0 all-gather.2.cloned.1.call-update
  208.1 75.4 %all-gather.2.cloned.1.call-done = f32[12288,2,128]{2,0,1:T(8,128)} async-done(((f32[768,2,128]{2,0,1:T(8,128)}), f32[12288,2,128]{2,0,1:T(8,128)}) %all-gather.2.cloned.1.call-update) | async-done | bytes 12582928 | tf_op jit(solution)/shard_map/all_gather | solution.py:65
  283.5 10.2 %convolution_bitcast_fusion = f32[2,32,128]{2,1,0:T(8,128)} fusion(f32[12288,2,128]{2,0,1:T(8,128)} %all-gather.2.cloned.1.call-done, f32[2,32,12288]{2,1,0:T(8,128)S(1)} %copy-done), kind=kOutput, calls=%fused_computation.1 | convolution fusion | flops 1207959552 | bytes 15761408 | tf_op jit(solution)/shard_map/krl,lkc->krc/dot_general | solution.py:62
  (4 shorter events, 0.0 us)
Async XLA Ops:
  6.5 2.0 copy-start
  6.5 159.8 %reduce-scatter.2.cloned.1.call-start = ((), (), s32[]{:S(2)}) async-start(), calls=%async_computation.1 | async-start | bytes 13369344 | tf_op jit(solution)/shard_map/reduce_scatter | solution.py:54
  8.5 12.6 %copy-start.1 = (f32[768,8,8]{0,2,1:T(8,128)S(1)}, f32[768,8,8]{0,2,1:T(8,128)}, u32[]{:S(2)}) copy-start(f32[768,8,8]{0,2,1:T(8,128)} %param.10) | copy-start | bytes 589828
  8.5 15.0 %copy-start.2 = (s32[2]{0:T(128)S(1)}, s32[2]{0:T(128)}, u32[]{:S(2)}) copy-start(s32[2]{0:T(128)} %param.13) | copy-start | bytes 28
  21.1 262.4 %all-gather.2.cloned.1.call-start = ((), (), s32[]{:S(2)}) async-start(), calls=%async_computation.2 | async-start | bytes 13369344 | tf_op jit(solution)/shard_map/all_gather | solution.py:65
Sparse Core Ops, SparseCore 0:
  21.2 145.0 reduce-scatter.1
  208.2 75.2 all-gather.1
where the time goes:
time: 301 us
  waiting for transfers between devices  187 us (62%)
  matrix products  40.3 us (13%)
  blocking collectives  30.7 us (10%)
  local copies, waits for them, and re-layouts  26.6 us (9%)
  between operations  13.4 us (4%)
    reduce_scatter x1, waiting for transfers between devices, body(): lax.psum_scatter(partial_running_sum.reshape(blocks * lax.axis_size('blk'...  112 us
    all_gather x1, waiting for transfers between devices, body(): lax.all_gather(scaled, 'blk', axis=0, tiled=True)  75.4 us
    psum x1, blocking collectives, finish(): response = lax.psum(response, 'blk')  30.7 us
    dot_general x1, matrix products, finish(): jnp.einsum('dvr,dotrq->dotvq', matched_filter_weights, masked_values, pre...  16.1 us
    dot_general x1, matrix products, body(): jnp.einsum('krl,krc->lkc', columns, injected, precision=highest_degree)  12.6 us
    mul x1, local copies, waits for them, and re-layouts, finish(): harmonics * kept_mask[:, :, None]  11.3 us
    dot_general x1, matrix products, body(): jnp.einsum('krl,lkc->krc', columns, lax.all_gather(scaled, 'blk', axis=0,...  10.2 us
    mul x1, local copies, waits for them, and re-layouts, finish(): scaled = matched_output * (L / jnp.sqrt(response))[None, :, None, :, None]  9.92 us
  transfers between devices with their start and end apart: 2, of which 2 were waited for; matrix products, arithmetic and copies ran while one was open for 1% of the time, Pallas kernels for 0%

commit v1 on v0

--- a/solution.py
+++ b/solution.py
@@ -1,3 +1,4 @@
+import functools
 import jax
 import jax.numpy as jnp
 from jax import lax
@@ -9,6 +10,18 @@
 SIMS = 8
 M = 2
 highest_degree = lax.Precision.HIGHEST
+
+
+def list_patches(panel, which_axis, row_dim):
+    entries = []
+    for _ in range(jax.lax.axis_size(which_axis)):
+        entries.append(panel)
+    outer = jnp.stack(entries)
+    current_value = jax.lax.all_to_all(outer, which_axis, 0, 0)
+    return jnp.concatenate(current_value, row_dim)
+
+
+remake_chunk = functools.partial(list_patches, which_axis="blk", row_dim=0)
 
 
 def inject(fourier_cycles, cycle_weight, cluster_cycles, cluster_flux):
@@ -59,12 +72,7 @@
     )
     scaled = finish(owned, matched_filter_weights, order_per_slot)
     columns = legendre
-    return jnp.einsum(
-        "krl,lkc->krc",
-        columns,
-        lax.all_gather(scaled, "blk", axis=0, tiled=True),
-        precision=highest_degree,
-    )
+    return jnp.einsum("krl,lkc->krc", columns, remake_chunk(scaled), precision=highest_degree)
 
 
 def solution(mesh):

time: 301 us -> 383 us (1.27)
  blocking collectives: 30.7 us -> 175 us
  waiting for transfers between devices: 187 us -> 112 us
  local copies, waits for them, and re-layouts: 26.6 us -> 39.5 us
    all_to_all x0 -> x1, blocking collectives: none -> 145 us  [list_patches(): current_value = jax.lax.all_to_all(outer, which_axis, 0, 0)]
    all_gather x1 -> x0, waiting for transfers between devices: 75.4 us -> none  [body(): lax.all_gather(scaled, 'blk', axis=0, tiled=True)]
    all_to_all x0 -> x1, local copies, waits for them, and re-layouts: none -> 10.4 us  [list_patches(): current_value = jax.lax.all_to_all(outer, which_axis, 0, 0)]
    another operation x0 -> x2, local copies, waits for them, and re-layouts: none -> 4.85 us  [list_patches(): outer = jnp.stack(entries)]
  transfers between devices with their start and end apart: 2 -> 1, of which waited for: 2 -> 1; matrix products, arithmetic and copies ran while one was open for 1% -> 1% of each run, Pallas kernels for 0% -> 0%
where the time goes in v1:
time: 383 us
  blocking collectives  175 us (46%)
  waiting for transfers between devices  112 us (29%)
  matrix products  40.2 us (10%)
  local copies, waits for them, and re-layouts  39.5 us (10%)
  between operations  13.4 us (3%)
    all_to_all x1, blocking collectives, list_patches(): current_value = jax.lax.all_to_all(outer, which_axis, 0, 0)  145 us
    reduce_scatter x1, waiting for transfers between devices, body(): lax.psum_scatter(partial_running_sum.reshape(blocks * lax.axis_size('blk'...  112 us
    psum x1, blocking collectives, finish(): response = lax.psum(response, 'blk')  30.5 us
    dot_general x1, matrix products, finish(): jnp.einsum('dvr,dotrq->dotvq', matched_filter_weights, masked_values, pre...  16.1 us
    dot_general x1, matrix products, body(): jnp.einsum('krl,krc->lkc', columns, injected, precision=highest_degree)  12.4 us
    mul x1, local copies, waits for them, and re-layouts, finish(): harmonics * kept_mask[:, :, None]  11.3 us
    all_to_all x1, local copies, waits for them, and re-layouts, list_patches(): current_value = jax.lax.all_to_all(outer, which_axis, 0, 0)  10.4 us
    dot_general x1, matrix products, body(): jnp.einsum('krl,lkc->krc', columns, remake_chunk(scaled), precision=highe...  10.2 us
  transfers between devices with their start and end apart: 1, of which 1 were waited for; matrix products, arithmetic and copies ran while one was open for 1% of the time, Pallas kernels for 0%

profile of v1, /device:TPU:1, one launch (start us, length us, event | category | flops | bytes accessed | tf_op | source)
XLA Modules:
  0.0 382.6 jit_solution(14891296175810559527)
XLA Ops:
  6.5 0.0 copy-start
  6.5 0.0 reduce-scatter.2.cloned.1.call-start
  6.5 1.2 fusion
  7.7 0.8 copy-done
  8.5 0.0 copy-start.1
  8.5 0.0 copy-start.2
  8.5 12.4 %fusion.10 = f32[2,128,12288]{2,1,0:T(8,128)} fusion(f32[2,32,128]{2,1,0:T(8,128)S(1)} %fusion, f32[2,32,12288]{2,1,0:T(8,128)S(1)} %copy-done), kind=kOutput, calls=%fused_computation.21 | convolution fusion | flops 1207959552 | bytes 15761408 | tf_op jit(solution)/shard_map/krl,krc->lkc/dot_general | solution.py:66
  20.9 0.0 reduce-scatter.2.cloned.1.call-update
  21.0 0.0 copy-done.1
  21.0 2.3 copy.18
  23.3 0.1 multiply_reduce_fusion
  23.3 0.0 copy-done.2
  23.3 0.2 fusion.4
  23.6 30.5 %psum.7 = f32[2,8]{1,0:T(2,128)S(1)} all-reduce(f32[2,8]{1,0:T(2,128)S(1)} %fusion.4), channel_id=1, replica_groups=mesh['order'=16,'blk'=16] {'blk'}, use_global_device_ids=true, to_apply=%region_2.0 | all-reduce | flops 16 | bytes 128 | tf_op jit(solution)/shard_map/psum | solution.py:47
  54.1 0.1 compare_convert_fusion
  54.2 112.0 %reduce-scatter.2.cloned.1.call-done = f32[768,256]{0,1:T(8,128)} async-done(((f32[12288,256]{0,1:T(8,128)}), f32[768,256]{0,1:T(8,128)}) %reduce-scatter.2.cloned.1.call-update) | async-done | bytes 786448 | tf_op jit(solution)/shard_map/reduce_scatter | solution.py:67
  166.2 2.1 broadcast_multiply_fusion
  168.3 11.3 %copy.13 = f32[768,2,2,8,8]{3,4,2,1,0:T(8,128)} copy(f32[768,2,2,8,8]{0,4,3,2,1:T(8,128)} %broadcast_multiply_fusion) | data formatting | bytes 1572864 | tf_op jit(solution)/shard_map/mul | solution.py:40
  179.6 16.1 %multiply_bitcast_fusion = f32[768,2,2,8,8]{3,4,2,1,0:T(8,128)} fusion(f32[2,8]{1,0:T(2,128)S(1)} %rsqrt_multiply_fusion, f32[768,2,2,8,8]{3,4,2,1,0:T(8,128)} %copy.13, f32[768,8,8,1,1]{2,1,4,3,0:T(8,128)} %copy.18), kind=kOutput, calls=%fused_computation | convolution fusion | flops 19070976 | bytes 1769536 | tf_op jit(solution)/shard_map/dvr,dotrq->dotvq/dot_general | solution.py:41
  195.7 9.9 %copy.15 = f32[768,2,2,8,8]{0,4,3,2,1:T(8,128)} copy(f32[768,2,2,8,8]{3,4,2,1,0:T(8,128)} %multiply_bitcast_fusion) | data formatting | bytes 1572864 | tf_op jit(solution)/shard_map/mul | solution.py:48
  205.6 2.3 copy.16
  207.9 2.5 stack.3
  210.5 144.7 %all_to_all.5 = f32[16,768,2,128]{3,1,2,0:T(8,128)} all-to-all(f32[16,768,2,128]{3,1,2,0:T(8,128)S(1)} %stack.3), channel_id=1, replica_groups=mesh['order'=16,'blk'=16] {'blk'}, dimensions={0} | all-to-all | bytes 25165824 | tf_op jit(solution)/shard_map/all_to_all | solution.py:20
  355.1 10.4 %copy.17 = f32[16,768,2,128]{3,1,0,2:T(8,128)} copy(f32[16,768,2,128]{3,1,2,0:T(8,128)} %all_to_all.5) | data formatting | bytes 25165824 | tf_op jit(solution)/shard_map/all_to_all | solution.py:20
  365.6 10.2 %convolution_bitcast_fusion = f32[2,32,128]{2,1,0:T(8,128)} fusion(f32[12288,2,128]{2,0,1:T(8,128)} %bitcast.19, f32[2,32,12288]{2,1,0:T(8,128)S(1)} %copy-done), kind=kOutput, calls=%fused_computation.1 | convolution fusion | flops 1207959552 | bytes 15761408 | tf_op jit(solution)/shard_map/krl,lkc->krc/dot_general | solution.py:75
  (4 shorter events, 0.0 us)
Async XLA Ops:
  6.5 2.0 copy-start
  6.5 159.7 %reduce-scatter.2.cloned.1.call-start = ((), (), s32[]{:S(2)}) async-start(), calls=%async_computation.2 | async-start | bytes 13369344 | tf_op jit(solution)/shard_map/reduce_scatter | solution.py:67
  8.5 12.5 %copy-start.1 = (f32[768,8,8]{0,2,1:T(8,128)S(1)}, f32[768,8,8]{0,2,1:T(8,128)}, u32[]{:S(2)}) copy-start(f32[768,8,8]{0,2,1:T(8,128)} %param.10) | copy-start | bytes 589828
  8.5 14.8 %copy-start.2 = (s32[2]{0:T(128)S(1)}, s32[2]{0:T(128)}, u32[]{:S(2)}) copy-start(s32[2]{0:T(128)} %param.13) | copy-start | bytes 28
Sparse Core Ops, SparseCore 0:
  21.1 145.0 reduce-scatter.1

commit v2 on v0

--- a/solution.py
+++ b/solution.py
@@ -9,6 +9,11 @@
 SIMS = 8
 M = 2
 highest_degree = lax.Precision.HIGHEST
+
+
+def gather_and_add(x, mesh_axis):
+    parts = lax.all_gather(x, mesh_axis)
+    return jnp.sum(parts, axis=0)
 
 
 def inject(fourier_cycles, cycle_weight, cluster_cycles, cluster_flux):
@@ -31,7 +36,7 @@
     squares = jnp.sum(matched_filter_weights * matched_filter_weights, axis=2)
     weights = kept_mask * (2.0 * degrees.astype(jnp.float32) + 1.0)[:, None]
     response = jnp.einsum("lk,ls->ks", weights, squares, precision=highest_degree)
-    response = lax.psum(response, "blk")
+    response = gather_and_add(response, "blk")
     scaled = matched_output * (L / jnp.sqrt(response))[None, :, None, :, None]
     return scaled.reshape(blocks, M, 2 * S * SIMS)
 

time: 301 us -> 300 us (level)
  blocking collectives: 30.7 us -> 21.6 us
  waiting for transfers between devices: 187 us -> 196 us
    psum x1 -> x0, blocking collectives: 30.7 us -> none  [finish(): response = lax.psum(response, 'blk')]
    all_gather x0 -> x1, blocking collectives: none -> 21.6 us  [gather_and_add(): parts = lax.all_gather(x, mesh_axis)]
    reduce_scatter x1, waiting for transfers between devices: 112 us -> 121 us  [body(): lax.psum_scatter(partial_running_sum.reshape(blocks * lax.axis_size('blk'...]
where the time goes in v2:
time: 300 us
  waiting for transfers between devices  196 us (65%)
  matrix products  40.3 us (13%)
  local copies, waits for them, and re-layouts  26.6 us (9%)
  blocking collectives  21.6 us (7%)
  between operations  13.4 us (4%)
    reduce_scatter x1, waiting for transfers between devices, body(): lax.psum_scatter(partial_running_sum.reshape(blocks * lax.axis_size('blk'...  121 us
    all_gather x1, waiting for transfers between devices, body(): lax.all_gather(scaled, 'blk', axis=0, tiled=True)  75.3 us
    all_gather x1, blocking collectives, gather_and_add(): parts = lax.all_gather(x, mesh_axis)  21.6 us
    dot_general x1, matrix products, finish(): jnp.einsum('dvr,dotrq->dotvq', matched_filter_weights, masked_values, pre...  16.1 us
    dot_general x1, matrix products, body(): jnp.einsum('krl,krc->lkc', columns, injected, precision=highest_degree)  12.6 us
    mul x1, local copies, waits for them, and re-layouts, finish(): harmonics * kept_mask[:, :, None]  11.3 us
    dot_general x1, matrix products, body(): jnp.einsum('krl,lkc->krc', columns, lax.all_gather(scaled, 'blk', axis=0,...  10.2 us
    mul x1, local copies, waits for them, and re-layouts, finish(): scaled = matched_output * (L / jnp.sqrt(response))[None, :, None, :, None]  9.92 us
  transfers between devices with their start and end apart: 2, of which 2 were waited for; matrix products, arithmetic and copies ran while one was open for 1% of the time, Pallas kernels for 0%

profile of v2, /device:TPU:1, one launch (start us, length us, event | category | flops | bytes accessed | tf_op | source)
XLA Modules:
  0.0 300.2 jit_solution(9863415770965442094)
XLA Ops:
  6.5 0.0 copy-start
  6.5 0.0 reduce-scatter.2.cloned.1.call-start
  6.5 1.2 fusion
  7.7 0.8 copy-done
  8.5 0.0 copy-start.1
  8.5 0.0 copy-start.2
  8.5 12.6 %fusion.9 = f32[2,128,12288]{2,1,0:T(8,128)} fusion(f32[2,32,128]{2,1,0:T(8,128)S(1)} %fusion, f32[2,32,12288]{2,1,0:T(8,128)S(1)} %copy-done), kind=kOutput, calls=%fused_computation.21 | convolution fusion | flops 1207959552 | bytes 15761408 | tf_op jit(solution)/shard_map/krl,krc->lkc/dot_general | solution.py:58
  21.1 0.0 reduce-scatter.2.cloned.1.call-update
  21.1 0.0 all-gather.4.cloned.1.call-start
  21.1 0.0 copy-done.1
  21.2 2.3 copy.17
  23.5 0.1 multiply_reduce_fusion
  23.5 0.0 copy-done.2
  23.5 0.2 convolution_bitcast_fusion.1
  23.7 21.6 %all-gather.1 = f32[16,2,8]{2,1,0:T(2,128)S(1)} all-gather(f32[1,2,8]{2,1,0:T(2,128)S(1)} %convolution_bitcast_fusion.1), channel_id=2, replica_groups=mesh['order'=16,'blk'=16] {'blk'}, dimensions={0}, use_global_device_ids=true | all-gather | bytes 1088 | tf_op jit(solution)/shard_map/all_gather | solution.py:15
  45.3 0.1 compare_convert_fusion
  45.4 120.6 %reduce-scatter.2.cloned.1.call-done = f32[768,256]{0,1:T(8,128)} async-done(((f32[12288,256]{0,1:T(8,128)}), f32[768,256]{0,1:T(8,128)}) %reduce-scatter.2.cloned.1.call-update) | async-done | bytes 786448 | tf_op jit(solution)/shard_map/reduce_scatter | solution.py:59
  166.0 2.1 broadcast_multiply_fusion
  168.1 11.3 %copy.13 = f32[768,2,2,8,8]{3,4,2,1,0:T(8,128)} copy(f32[768,2,2,8,8]{0,4,3,2,1:T(8,128)} %broadcast_multiply_fusion) | data formatting | bytes 1572864 | tf_op jit(solution)/shard_map/mul | solution.py:32
  179.4 16.1 %multiply_bitcast_fusion = f32[768,2,2,8,8]{3,4,2,1,0:T(8,128)} fusion(f32[2,8]{1,0:T(2,128)S(1)} %rsqrt_multiply_fusion, f32[768,2,2,8,8]{3,4,2,1,0:T(8,128)} %copy.13, f32[768,8,8,1,1]{2,1,4,3,0:T(8,128)} %copy.17), kind=kOutput, calls=%fused_computation | convolution fusion | flops 19070976 | bytes 1769536 | tf_op jit(solution)/shard_map/dvr,dotrq->dotvq/dot_general | solution.py:33
  195.5 9.9 %copy.15 = f32[768,2,2,8,8]{0,4,3,2,1:T(8,128)} copy(f32[768,2,2,8,8]{3,4,2,1,0:T(8,128)} %multiply_bitcast_fusion) | data formatting | bytes 1572864 | tf_op jit(solution)/shard_map/mul | solution.py:40
  205.4 2.3 copy.16
  207.8 0.0 all-gather.4.cloned.1.call-update
  207.8 75.3 %all-gather.4.cloned.1.call-done = f32[12288,2,128]{2,0,1:T(8,128)} async-done(((f32[768,2,128]{2,0,1:T(8,128)}), f32[12288,2,128]{2,0,1:T(8,128)}) %all-gather.4.cloned.1.call-update) | async-done | bytes 12582928 | tf_op jit(solution)/shard_map/all_gather | solution.py:70
  283.1 10.2 %convolution_bitcast_fusion = f32[2,32,128]{2,1,0:T(8,128)} fusion(f32[12288,2,128]{2,0,1:T(8,128)} %all-gather.4.cloned.1.call-done, f32[2,32,12288]{2,1,0:T(8,128)S(1)} %copy-done), kind=kOutput, calls=%fused_computation.1 | convolution fusion | flops 1207959552 | bytes 15761408 | tf_op jit(solution)/shard_map/krl,lkc->krc/dot_general | solution.py:67
  (5 shorter events, 0.0 us)
Async XLA Ops:
  6.5 2.0 copy-start
  6.5 159.5 %reduce-scatter.2.cloned.1.call-start = ((), (), s32[]{:S(2)}) async-start(), calls=%async_computation.1 | async-start | bytes 13369344 | tf_op jit(solution)/shard_map/reduce_scatter | solution.py:59
  8.5 12.6 %copy-start.1 = (f32[768,8,8]{0,2,1:T(8,128)S(1)}, f32[768,8,8]{0,2,1:T(8,128)}, u32[]{:S(2)}) copy-start(f32[768,8,8]{0,2,1:T(8,128)} %param.10) | copy-start | bytes 589828
  8.5 15.0 %copy-start.2 = (s32[2]{0:T(128)S(1)}, s32[2]{0:T(128)}, u32[]{:S(2)}) copy-start(s32[2]{0:T(128)} %param.13) | copy-start | bytes 28
  21.1 262.0 %all-gather.4.cloned.1.call-start = ((), (), s32[]{:S(2)}) async-start(), calls=%async_computation.2 | async-start | bytes 13369344 | tf_op jit(solution)/shard_map/all_gather | solution.py:70
Sparse Core Ops, SparseCore 0:
  21.2 144.7 reduce-scatter.1
  207.9 75.1 all-gather.3
